TPU v7x, 32 devices: a whole 2x2x4 slice. The times are simulated.
32 devices in a mesh: seq: 16 (over z, x, core), tp: 2 (over y).
Axes of the slice: x: 2, y: 2, z: 4, core: 2. Of those that a mesh axis runs over, the one named last changes fastest.
Arguments:
- tokens: bfloat16 [2048, 5120], P('seq', 'tp'), may hold values from -4 to 4
- self_queries: bfloat16 [2048, 3072], P('seq', 'tp'), may hold values from -12 to 12
- self_keys: bfloat16 [2048, 3072], P('seq', 'tp'), may hold values from -12 to 12
- self_values: bfloat16 [2048, 3072], P('seq', 'tp'), may hold values from -6 to 6
- cross_queries: bfloat16 [2048, 3072], P('seq', 'tp'), may hold values from -12 to 12
- caption_keys: bfloat16 [512, 3072], P('seq', 'tp'), may hold values from -12 to 12
- caption_values: bfloat16 [512, 3072], P('seq', 'tp'), may hold values from -6 to 6
- out_weight: bfloat16 [3072, 5120], P('tp'), may hold values from -0.15625 to 0.15625
- gate_vector: float32 [5120], P('tp'), may hold values from -6 to 6
Outputs:
- updated: bfloat16 [2048, 5120], P('seq', 'tp')
- cross_heads: bfloat16 [2048, 3072], P('seq', 'tp')
All inputs are finite; a program needn't handle non-finite values.
Results may differ from a plain program's by a relative error of at most 0.0085.
Values may be sent and summed in bfloat16 or wider, within the bound.
No kernel may reach another device: no remote copies, remote signals or barrier semaphores. Data moves between devices by JAX's collectives and lax.ppermute only.
A program may use at most 128 MiB of HBM per device.

v0:
```python
import math
import jax
import jax.numpy as jnp
from jax import lax
from jax.sharding import PartitionSpec as P

DH = 128


def online_step(running, pieces, query_split, score_scale):
    maxima, totals, accum = running
    keys_piece, values_piece = pieces
    row_count = keys_piece.shape[0]
    heads_here = query_split.shape[1]
    keys_split = keys_piece.reshape(row_count, heads_here, DH)
    values_split = values_piece.reshape(row_count, heads_here, DH)
    scores = (
        jnp.einsum("thd,khd->thk", query_split, keys_split, preferred_element_type=jnp.float32)
        * score_scale
    )
    new_max = jnp.maximum(maxima, jnp.max(scores, axis=2))
    rescale = jnp.exp(maxima - new_max)
    exp_scores = jnp.exp(scores - new_max[:, :, None])
    totals = totals * rescale + jnp.sum(exp_scores, axis=2)
    weights = exp_scores.astype(jnp.bfloat16)
    accum = accum * rescale[:, :, None] + jnp.einsum(
        "thk,khd->thd", weights, values_split, preferred_element_type=jnp.float32
    )
    return (new_max, totals, accum)


def bounded_step(running, pieces, query_split, score_scale):
    row_count = pieces[0].shape[0]
    block_rows = math.gcd(row_count, 1024)
    if block_rows == row_count:
        return online_step(running, pieces, query_split, score_scale)

    def loop_body(position, current):
        keys_piece = lax.dynamic_slice_in_dim(pieces[0], position * block_rows, block_rows, 0)
        values_piece = lax.dynamic_slice_in_dim(pieces[1], position * block_rows, block_rows, 0)
        return online_step(current, (keys_piece, values_piece), query_split, score_scale)

    return lax.fori_loop(0, row_count // block_rows, loop_body, running)


def initial_state(row_count, heads_here):
    return (
        jnp.full((row_count, heads_here), -1e30, jnp.float32),
        jnp.zeros((row_count, heads_here), jnp.float32),
        jnp.zeros((row_count, heads_here, DH), jnp.float32),
    )


def finish(running):
    maxima, totals, accum = running
    row_count, heads_here = totals.shape
    return (accum / totals[:, :, None]).reshape(row_count, heads_here * DH).astype(jnp.bfloat16)


def shards(
    tokens,
    self_queries,
    self_keys,
    self_values,
    cross_queries,
    caption_keys,
    caption_values,
    out_weight,
    gate_vector,
):
    row_count = self_queries.shape[0]
    heads_here = self_queries.shape[1] // DH
    score_scale = 1.0 / math.sqrt(DH)
    self_split = self_queries.reshape(row_count, heads_here, DH)
    cross_split = cross_queries.reshape(row_count, heads_here, DH)
    self_state = bounded_step(
        initial_state(row_count, heads_here),
        (
            lax.all_gather(self_keys, "seq", axis=0, tiled=True),
            lax.all_gather(self_values, "seq", axis=0, tiled=True),
        ),
        self_split,
        score_scale,
    )
    self_heads = finish(self_state)
    caption_all = (
        lax.all_gather(caption_keys, "seq", axis=0, tiled=True),
        lax.all_gather(caption_values, "seq", axis=0, tiled=True),
    )
    cross_state = bounded_step(
        initial_state(row_count, heads_here), caption_all, cross_split, score_scale
    )
    cross_heads = finish(cross_state)
    partial_terms = jnp.dot(self_heads, out_weight, preferred_element_type=jnp.float32)
    projected = lax.psum_scatter(
        partial_terms.astype(jnp.bfloat16), "tp", scatter_dimension=1, tiled=True
    ).astype(jnp.float32)
    updated = (tokens.astype(jnp.float32) + gate_vector[None, :] * projected).astype(jnp.bfloat16)
    return (updated, cross_heads)


def solution(mesh):
    return jax.shard_map(
        shards,
        mesh=mesh,
        in_specs=(
            P("seq", "tp"),
            P("seq", "tp"),
            P("seq", "tp"),
            P("seq", "tp"),
            P("seq", "tp"),
            P("seq", "tp"),
            P("seq", "tp"),
            P("tp", None),
            P("tp"),
        ),
        out_specs=(P("seq", "tp"), P("seq", "tp")),
        check_vma=False,
    )
```

profile of v0, /device:TPU:0, one launch (start us, length us, event | category | flops | bytes accessed | tf_op | source)
XLA Modules:
  0.0 259.5 jit_solution(5244744670284265529)
XLA Ops:
  7.2 1.9 copy.32
  9.2 1.9 copy.34
  12.5 1.2 copy.33
  14.0 65.1 %all-gather.5.cloned.1.call-done = bf16[2048,1536]{0,1:T(8,128)(2,1)} async-done(((bf16[128,1536]{0,1:T(8,128)(2,1)}), bf16[2048,1536]{0,1:T(8,128)(2,1)}) %all-gather.5.cloned.1.call-update) | async-done | bytes 6291472 | tf_op jit(solution)/shard_map/all_gather | solution.py:79
  79.1 66.6 %all-gather.7.cloned.1.call-done = bf16[2048,1536]{0,1:T(8,128)(2,1)} async-done(((bf16[128,1536]{0,1:T(8,128)(2,1)}), bf16[2048,1536]{0,1:T(8,128)(2,1)}) %all-gather.7.cloned.1.call-update) | async-done | bytes 6291472 | tf_op jit(solution)/shard_map/all_gather | solution.py:80
  145.7 30.5 %while.18 = (s32[]{:T(128)}, f32[128,12]{0,1:T(8,128)S(1)}, f32[128,12]{0,1:T(8,128)}, f32[128,12,128]{0,2,1:T(8,128)}, bf16[2048,1536]{0,1:T(8,128)(2,1)}, /*in...) while((s32[]{:T(128)}, f32[128,12]{0,1:T(8,128)S(1)}, ...), condition=%wide.region_3.0_spmd.clone, body=%wide.region_0.0_spmd.clone.sunk | while | flops 818486784 | bytes 65028356 | solution.py:43
  145.7 3.6 %constant_dynamic-slice_fusion.3 = (bf16[1024,1536]{0,1:T(8,128)(2,1)S(1)}, bf16[1024,1536]{0,1:T(8,128)(2,1)S(1)}) fusion(bf16[2048,1536]{0,1:T(8,128)(2,1)} %get-tuple-element.280, s32[]{:T(128)S(6)} %select_n.10, bf16[2048,1536]{0,1:T(8,128)(2,1)} %get-tuple-element.278), kind=kLoop, calls=%fused_computation.15.clone.1 | loop fusion | bytes 12582916 | tf_op jit(solution)/shard_map/while/body/eval_jaxpr/dynamic_slice | solution.py:40
  149.3 3.8 %bitcast_reduce_fusion.3 = (f32[128,12]{0,1:T(8,128)S(1)}, f32[12,1024,128]{2,1,0:T(8,128)}) fusion(bf16[1024,12,128]{0,2,1:T(8,128)(2,1)S(1)} %bitcast.79, bf16[128,12,128]{2,0,1:T(8,128)(2,1)S(1)} %get-tuple-element.279), kind=kOutput, calls=%fused_computation.1.clone.1 | convolution fusion | flops 405797376 | bytes 9836544 | tf_op jit(solution)/shard_map/while/body/eval_jaxpr/thd,khd->thk/dot_general | solution.py:18
  153.1 4.0 %fusion.55 = f32[128,12]{0,1:T(8,128)S(1)} fusion(f32[12,1024,128]{2,1,0:T(8,128)} %get-tuple-element.248, f32[128,12]{0,1:T(8,128)S(1)} %select_maximum_fusion.2), kind=kLoop, calls=%fused_computation.4.clone.1 | loop fusion | flops 4717056 | bytes 6303744 | tf_op jit(solution)/shard_map/while/body/eval_jaxpr/reduce_sum | solution.py:24
  157.8 2.5 fusion.57
  160.4 3.6 %constant_dynamic-slice_fusion.3 = (bf16[1024,1536]{0,1:T(8,128)(2,1)S(1)}, bf16[1024,1536]{0,1:T(8,128)(2,1)S(1)}) fusion(bf16[2048,1536]{0,1:T(8,128)(2,1)} %get-tuple-element.280, s32[]{:T(128)S(6)} %select_n.10, bf16[2048,1536]{0,1:T(8,128)(2,1)} %get-tuple-element.278), kind=kLoop, calls=%fused_computation.15.clone.1 | loop fusion | bytes 12582916 | tf_op jit(solution)/shard_map/while/body/eval_jaxpr/dynamic_slice | solution.py:40
  163.9 3.8 %bitcast_reduce_fusion.3 = (f32[128,12]{0,1:T(8,128)S(1)}, f32[12,1024,128]{2,1,0:T(8,128)}) fusion(bf16[1024,12,128]{0,2,1:T(8,128)(2,1)S(1)} %bitcast.79, bf16[128,12,128]{2,0,1:T(8,128)(2,1)S(1)} %get-tuple-element.279), kind=kOutput, calls=%fused_computation.1.clone.1 | convolution fusion | flops 405797376 | bytes 9836544 | tf_op jit(solution)/shard_map/while/body/eval_jaxpr/thd,khd->thk/dot_general | solution.py:18
  167.8 4.0 %fusion.55 = f32[128,12]{0,1:T(8,128)S(1)} fusion(f32[12,1024,128]{2,1,0:T(8,128)} %get-tuple-element.248, f32[128,12]{0,1:T(8,128)S(1)} %select_maximum_fusion.2), kind=kLoop, calls=%fused_computation.4.clone.1 | loop fusion | flops 4717056 | bytes 6303744 | tf_op jit(solution)/shard_map/while/body/eval_jaxpr/reduce_sum | solution.py:24
  171.8 0.8 copy-done
  172.6 3.7 %fusion.57 = f32[128,12,128]{0,2,1:T(8,128)} fusion(bf16[1024,12,128]{0,2,1:T(8,128)(2,1)S(1)} %bitcast.78, f32[12,1024,128]{2,1,0:T(8,128)S(1)} %copy-done, f32[128,12]{0,1:T(8,128)S(1)} %select_maximum_fusion.2, f32[128,12,128]{0,2,1:T(8,128)} %get-tuple-element.266, f32[128,12]{0,1:T(8,128)S(1)} %get-tuple-element.251, pred[]{:T(512)S(6)} %compare.3), kind=kOutput, calls=%fused_computation.9.clone.1 | convolution fusion | flops 407961600 | bytes 11022337 | tf_op jit(solution)/shard_map/while/body/eval_jaxpr/thk,khd->thd/dot_general | solution.py:26
  176.2 1.2 divide_convert_fusion
  177.5 9.0 %convolution_convert_fusion = bf16[128,5120]{1,0:T(8,128)(2,1)} fusion(bf16[128,1536]{0,1:T(8,128)(2,1)S(1)} %bitcast.81, bf16[1536,5120]{1,0:T(8,128)(2,1)} %param.18), kind=kOutput, calls=%fused_computation.18 | convolution fusion | flops 2013921280 | bytes 17432576 | tf_op jit(solution)/shard_map/dot_general | solution.py:94
  186.8 1.7 copy.40
  188.5 38.1 %all-gather.9.cloned.1.call-done = bf16[512,1536]{1,0:T(8,128)(2,1)} async-done(((bf16[32,1536]{1,0:T(8,128)(2,1)}), bf16[512,1536]{1,0:T(8,128)(2,1)}) %all-gather.9.cloned.1.call-update) | async-done | bytes 1572880 | tf_op jit(solution)/shard_map/all_gather | solution.py:87
  226.6 1.7 copy.36
  229.6 0.9 fusion.31
  230.5 0.9 copy.42
  231.4 19.4 %reduce-scatter.2.cloned.1.call-done = bf16[128,2560]{1,0:T(8,128)(2,1)} async-done(((bf16[128,5120]{1,0:T(8,128)(2,1)}), bf16[128,2560]{1,0:T(8,128)(2,1)}) %reduce-scatter.2.cloned.1.call-update) | async-done | bytes 655376 | tf_op jit(solution)/shard_map/reduce_scatter | solution.py:95
  250.9 2.1 add_convert_fusion
  (43 shorter events, 3.8 us)
Async XLA Ops:
  7.2 72.0 %all-gather.5.cloned.1.call-start = ((), (), s32[]{:S(2)}) async-start(), calls=%async_computation.1 | async-start | bytes 6684672 | tf_op jit(solution)/shard_map/all_gather | solution.py:79
  9.1 136.6 %all-gather.7.cloned.1.call-start = ((), (), s32[]{:S(2)}) async-start(), calls=%async_computation.2 | async-start | bytes 6684672 | tf_op jit(solution)/shard_map/all_gather | solution.py:80
  11.1 175.6 %all-gather.11.cloned.1.call-start = ((), (), s32[]{:S(2)}) async-start(), calls=%async_computation.5 | async-start | bytes 1671168 | tf_op jit(solution)/shard_map/all_gather | solution.py:88
  11.9 214.8 %all-gather.9.cloned.1.call-start = ((), (), s32[]{:S(2)}) async-start(), calls=%async_computation.4 | async-start | bytes 1671168 | tf_op jit(solution)/shard_map/all_gather | solution.py:87
  12.5 238.4 %reduce-scatter.2.cloned.1.call-start = ((), (), s32[]{:S(2)}) async-start(), calls=%async_computation.3 | async-start | bytes 1966080 | tf_op jit(solution)/shard_map/reduce_scatter | solution.py:95
  153.1 4.0 %copy-start.3 = (f32[128,12]{0,1:T(8,128)S(1)}, f32[128,12]{0,1:T(8,128)}, u32[]{:S(2)}) copy-start(f32[128,12]{0,1:T(8,128)} %get-tuple-element.265) | copy-start | bytes 18436 | tf_op jit(solution)/shard_map/while
  153.1 4.7 %copy-start = (f32[12,1024,128]{2,1,0:T(8,128)S(1)}, f32[12,1024,128]{2,1,0:T(8,128)}, u32[]{:S(2)}) copy-start(f32[12,1024,128]{2,1,0:T(8,128)} %get-tuple-element.248) | copy-start | bytes 18874372 | tf_op jit(solution)/shard_map/while
  157.2 3.2 %copy-start.4 = (f32[128,12]{0,1:T(8,128)}, f32[128,12]{0,1:T(8,128)S(1)}, u32[]{:S(2)}) copy-start(f32[128,12]{0,1:T(8,128)S(1)} %get-tuple-element.276) | copy-start | bytes 18436 | tf_op jit(solution)/shard_map/while
  167.8 4.0 %copy-start.3 = (f32[128,12]{0,1:T(8,128)S(1)}, f32[128,12]{0,1:T(8,128)}, u32[]{:S(2)}) copy-start(f32[128,12]{0,1:T(8,128)} %get-tuple-element.265) | copy-start | bytes 18436 | tf_op jit(solution)/shard_map/while
  167.8 4.8 %copy-start = (f32[12,1024,128]{2,1,0:T(8,128)S(1)}, f32[12,1024,128]{2,1,0:T(8,128)}, u32[]{:S(2)}) copy-start(f32[12,1024,128]{2,1,0:T(8,128)} %get-tuple-element.248) | copy-start | bytes 18874372 | tf_op jit(solution)/shard_map/while
  171.8 4.5 %copy-start.4 = (f32[128,12]{0,1:T(8,128)}, f32[128,12]{0,1:T(8,128)S(1)}, u32[]{:S(2)}) copy-start(f32[128,12]{0,1:T(8,128)S(1)} %get-tuple-element.276) | copy-start | bytes 18436 | tf_op jit(solution)/shard_map/while
  177.5 9.0 %copy-start.2 = (bf16[128,1536]{1,0:T(8,128)(2,1)S(1)}, bf16[128,1536]{1,0:T(8,128)(2,1)}, u32[]{:S(2)}) copy-start(bf16[128,1536]{1,0:T(8,128)(2,1)} %param.15) | copy-start | bytes 1179652
  229.6 21.2 %copy-start.1 = (bf16[128,2560]{1,0:T(8,128)(2,1)S(1)}, bf16[128,2560]{1,0:T(8,128)(2,1)}, u32[]{:S(2)}) copy-start(bf16[128,2560]{1,0:T(8,128)(2,1)} %param.11) | copy-start | bytes 1966084
  229.6 21.2 %copy-start.5 = (f32[2560]{0:T(1024)S(1)}, f32[2560]{0:T(1024)}, u32[]{:S(2)}) copy-start(f32[2560]{0:T(1024)} %param.19) | copy-start | bytes 30724
Sparse Core Ops, SparseCore 0:
  10.7 68.3 all-gather.4
  81.9 63.8 all-gather.6
  148.0 37.8 all-gather.10
  188.0 38.5 all-gather.8
  228.7 22.0 reduce-scatter.1
where the time goes:
time: 260 us
  waiting for transfers between devices  191 us (73%)
  matrix products  24.4 us (9%)
  local copies, waits for them, and re-layouts  18.4 us (7%)
  between operations  13.9 us (5%)
  other arithmetic  11.9 us (5%)
    all_gather x1, waiting for transfers between devices, shards(): lax.all_gather(self_values, 'seq', axis=0, tiled=True)  66.6 us
    all_gather x1, waiting for transfers between devices, shards(): lax.all_gather(self_keys, 'seq', axis=0, tiled=True)  65.1 us
    all_gather x1, waiting for transfers between devices, shards(): lax.all_gather(caption_keys, 'seq', axis=0, tiled=True)  38.1 us
    reduce_scatter x1, waiting for transfers between devices, shards(): lax.psum_scatter(partial_terms.astype(jnp.bfloat16), 'tp', scatter_dimens...  19.4 us
    dot_general x1, matrix products, shards(): jnp.dot(self_heads, out_weight, preferred_element_type=jnp.float32)  8.99 us
    reduce_sum x3, other arithmetic, online_step(): totals = totals * rescale + jnp.sum(exp_scores, axis=2)  8.54 us
    dot_general x3, matrix products, online_step(): jnp.einsum('thd,khd->thk', query_split, keys_split, preferred_element_typ...  8.36 us
    dynamic_slice x2, local copies, waits for them, and re-layouts, loop_body(): lax.dynamic_slice_in_dim(pieces[1], position * block_rows, block_rows, 0)  7.11 us
  transfers between devices with their start and end apart: 5, of which 4 were waited for; matrix products, arithmetic and copies ran while one was open for 19% of the time, Pallas kernels for 0%

commit v1 on v0

--- a/solution.py
+++ b/solution.py
@@ -5,6 +5,18 @@
 from jax.sharding import PartitionSpec as P
 
 DH = 128
+
+
+def doubled_up(array, axis, dim):
+    ways, here, hop = (lax.axis_size(axis), lax.axis_index(axis), array.shape[dim])
+    line, have = (array, 1)
+    while have < ways:
+        line = jnp.concatenate(
+            [line, lax.ppermute(line, axis, [(d, (d - have) % ways) for d in range(ways)])],
+            axis=dim,
+        )
+        have = 2 * have
+    return jnp.roll(line, here * hop, axis=dim)
 
 
 def online_step(running, pieces, query_split, score_scale):
@@ -84,7 +96,7 @@
     )
     self_heads = finish(self_state)
     caption_all = (
-        lax.all_gather(caption_keys, "seq", axis=0, tiled=True),
+        doubled_up(caption_keys, "seq", 0),
         lax.all_gather(caption_values, "seq", axis=0, tiled=True),
     )
     cross_state = bounded_step(

time: 260 us -> 265 us (1.019)
  waiting for transfers between devices: 191 us -> 173 us
  starting transfers between devices: 0.2 us -> 9.23 us
  local copies, waits for them, and re-layouts: 18.4 us -> 25.8 us
  other arithmetic: 11.9 us -> 15.7 us
    ppermute x0 -> x4, waiting for transfers between devices: none -> 52.7 us  [doubled_up(): lax.ppermute(line, axis, [(d, (d - have) % ways) for d in range(ways)])]
    all_gather x1 -> x0, waiting for transfers between devices: 38.1 us -> none  [shards(): lax.all_gather(caption_keys, 'seq', axis=0, tiled=True)]
    reduce_scatter x1, waiting for transfers between devices: 19.4 us -> 0.01 us  [shards(): lax.psum_scatter(partial_terms.astype(jnp.bfloat16), 'tp', scatter_dimens...]
    all_gather x1, waiting for transfers between devices: 65.1 us -> 53.9 us  [shards(): lax.all_gather(self_keys, 'seq', axis=0, tiled=True)]
    ppermute x0 -> x4, starting transfers between devices: none -> 9.07 us  [doubled_up(): lax.ppermute(line, axis, [(d, (d - have) % ways) for d in range(ways)])]
    concatenate x0 -> x1, local copies, waits for them, and re-layouts: none -> 5.89 us  [doubled_up(): return jnp.roll(line, here * hop, axis=dim)]
    concatenate x0 -> x3, other arithmetic: none -> 3.01 us  [doubled_up(): jnp.concatenate([line, lax.ppermute(line, axis, [(d, (d - have) % ways) f...]
    unnamed x12 -> x23, local copies, waits for them, and re-layouts: 6.44 us -> 6.62 us
  transfers between devices with their start and end apart: 5 -> 8, of which waited for: 4 -> 5; matrix products, arithmetic and copies ran while one was open for 19% -> 23% of each run, Pallas kernels for 0% -> 0%
where the time goes in v1:
time: 265 us; the launch traced here: 264 us
  waiting for transfers between devices  173 us (65%)
  local copies, waits for them, and re-layouts  25.8 us (10%)
  matrix products  25.8 us (10%)
  other arithmetic  15.7 us (6%)
  between operations  14 us (5%)
  starting transfers between devices  9.23 us (3%)
    all_gather x1, waiting for transfers between devices, shards(): lax.all_gather(self_values, 'seq', axis=0, tiled=True)  66.6 us
    all_gather x1, waiting for transfers between devices, shards(): lax.all_gather(self_keys, 'seq', axis=0, tiled=True)  53.9 us
    ppermute x4, waiting for transfers between devices, doubled_up(): lax.ppermute(line, axis, [(d, (d - have) % ways) for d in range(ways)])  52.7 us
    ppermute x4, starting transfers between devices, doubled_up(): lax.ppermute(line, axis, [(d, (d - have) % ways) for d in range(ways)])  9.07 us
    dot_general x1, matrix products, shards(): jnp.dot(self_heads, out_weight, preferred_element_type=jnp.float32)  9.01 us
    reduce_sum x3, other arithmetic, online_step(): totals = totals * rescale + jnp.sum(exp_scores, axis=2)  8.52 us
    dot_general x3, matrix products, online_step(): jnp.einsum('thk,khd->thd', weights, values_split, preferred_element_type=...  8.44 us
    dot_general x3, matrix products, online_step(): jnp.einsum('thd,khd->thk', query_split, keys_split, preferred_element_typ...  8.39 us
  transfers between devices with their start and end apart: 8, of which 5 were waited for; matrix products, arithmetic and copies ran while one was open for 23% of the time, Pallas kernels for 0%

profile of v1, /device:TPU:0, one launch (start us, length us, event | category | flops | bytes accessed | tf_op | source)
XLA Modules:
  0.0 263.9 jit_solution(9606974078511208315)
XLA Ops:
  7.2 2.0 copy.19
  9.2 1.9 copy.21
  12.4 5.5 %collective-permute-start = (bf16[32,1536]{0,1:T(8,128)(2,1)S(1)}, bf16[32,1536]{0,1:T(8,128)(2,1)S(1)}, u32[]{:S(2)}, u32[]{:S(2)}) collective-permute-start(bf16[32,1536]{0,1:T(8,128)(2,1)S(1)} %copy.27), channel_id=1, source_target_pairs={{0,30},{2,0},{4,2},{6,4},{8,6},{10,8},{12,10},{14,12},{16,14},{18,... | collective-permute-start | bytes 294920 | tf_op jit(solution)/shard_map/ppermute | solution.py:15
  17.8 7.0 %collective-permute-done = bf16[32,1536]{0,1:T(8,128)(2,1)S(1)} collective-permute-done((bf16[32,1536]{0,1:T(8,128)(2,1)S(1)}, bf16[32,1536]{0,1:T(8,128)(2,1)S(1)}, u32[]{:S(2)}, u32[]{:S(2)}) %collective-permute-start) | collective-permute-done | bytes 98336 | tf_op jit(solution)/shard_map/ppermute | solution.py:15
  25.7 11.1 %collective-permute-done.1 = bf16[64,1536]{0,1:T(8,128)(2,1)S(1)} collective-permute-done((bf16[64,1536]{0,1:T(8,128)(2,1)S(1)}, bf16[64,1536]{0,1:T(8,128)(2,1)S(1)}, u32[]{:S(2)}, u32[]{:S(2)}) %collective-permute-start.1) | collective-permute-done | bytes 196640 | tf_op jit(solution)/shard_map/ppermute | solution.py:15
  37.9 1.9 collective-permute-start.2
  39.8 53.9 %all-gather.4.cloned.1.call-done = bf16[2048,1536]{0,1:T(8,128)(2,1)} async-done(((bf16[128,1536]{0,1:T(8,128)(2,1)}), bf16[2048,1536]{0,1:T(8,128)(2,1)}) %all-gather.4.cloned.1.call-update) | async-done | bytes 6291472 | tf_op jit(solution)/shard_map/all_gather | solution.py:91
  93.8 66.6 %all-gather.6.cloned.1.call-done = bf16[2048,1536]{0,1:T(8,128)(2,1)} async-done(((bf16[128,1536]{0,1:T(8,128)(2,1)}), bf16[2048,1536]{0,1:T(8,128)(2,1)}) %all-gather.6.cloned.1.call-update) | async-done | bytes 6291472 | tf_op jit(solution)/shard_map/all_gather | solution.py:92
  160.4 30.4 %while.18 = (s32[]{:T(128)}, f32[128,12]{0,1:T(8,128)S(1)}, f32[128,12]{0,1:T(8,128)}, f32[128,12,128]{0,2,1:T(8,128)}, bf16[2048,1536]{0,1:T(8,128)(2,1)}, /*in...) while((s32[]{:T(128)}, f32[128,12]{0,1:T(8,128)S(1)}, ...), condition=%wide.region_3.0_spmd.clone, body=%wide.region_0.0_spmd.clone.sunk | while | flops 818486784 | bytes 65028356 | solution.py:55
  160.4 3.6 %constant_dynamic-slice_fusion.4 = (bf16[1024,1536]{0,1:T(8,128)(2,1)S(1)}, bf16[1024,1536]{0,1:T(8,128)(2,1)S(1)}) fusion(bf16[2048,1536]{0,1:T(8,128)(2,1)} %get-tuple-element.271, s32[]{:T(128)S(6)} %select_n.25, bf16[2048,1536]{0,1:T(8,128)(2,1)} %get-tuple-element.269), kind=kLoop, calls=%fused_computation.15.clone.1 | loop fusion | bytes 12582916 | tf_op jit(solution)/shard_map/while/body/eval_jaxpr/dynamic_slice | solution.py:52
  163.9 3.8 %bitcast_reduce_fusion.3 = (f32[128,12]{0,1:T(8,128)S(1)}, f32[12,1024,128]{2,1,0:T(8,128)}) fusion(bf16[1024,12,128]{0,2,1:T(8,128)(2,1)S(1)} %bitcast.79, bf16[128,12,128]{2,0,1:T(8,128)(2,1)S(1)} %get-tuple-element.270), kind=kOutput, calls=%fused_computation.1.clone.1 | convolution fusion | flops 405797376 | bytes 9836544 | tf_op jit(solution)/shard_map/while/body/eval_jaxpr/thd,khd->thk/dot_general | solution.py:30
  167.8 4.0 %fusion.55 = f32[128,12]{0,1:T(8,128)S(1)} fusion(f32[12,1024,128]{2,1,0:T(8,128)} %get-tuple-element.239, f32[128,12]{0,1:T(8,128)S(1)} %select_maximum_fusion.2), kind=kLoop, calls=%fused_computation.4.clone.1 | loop fusion | flops 4717056 | bytes 6303744 | tf_op jit(solution)/shard_map/while/body/eval_jaxpr/reduce_sum | solution.py:36
  172.5 2.5 fusion.57
  175.0 3.6 %constant_dynamic-slice_fusion.4 = (bf16[1024,1536]{0,1:T(8,128)(2,1)S(1)}, bf16[1024,1536]{0,1:T(8,128)(2,1)S(1)}) fusion(bf16[2048,1536]{0,1:T(8,128)(2,1)} %get-tuple-element.271, s32[]{:T(128)S(6)} %select_n.25, bf16[2048,1536]{0,1:T(8,128)(2,1)} %get-tuple-element.269), kind=kLoop, calls=%fused_computation.15.clone.1 | loop fusion | bytes 12582916 | tf_op jit(solution)/shard_map/while/body/eval_jaxpr/dynamic_slice | solution.py:52
  178.5 3.8 %bitcast_reduce_fusion.3 = (f32[128,12]{0,1:T(8,128)S(1)}, f32[12,1024,128]{2,1,0:T(8,128)}) fusion(bf16[1024,12,128]{0,2,1:T(8,128)(2,1)S(1)} %bitcast.79, bf16[128,12,128]{2,0,1:T(8,128)(2,1)S(1)} %get-tuple-element.270), kind=kOutput, calls=%fused_computation.1.clone.1 | convolution fusion | flops 405797376 | bytes 9836544 | tf_op jit(solution)/shard_map/while/body/eval_jaxpr/thd,khd->thk/dot_general | solution.py:30
  182.4 4.0 %fusion.55 = f32[128,12]{0,1:T(8,128)S(1)} fusion(f32[12,1024,128]{2,1,0:T(8,128)} %get-tuple-element.239, f32[128,12]{0,1:T(8,128)S(1)} %select_maximum_fusion.2), kind=kLoop, calls=%fused_computation.4.clone.1 | loop fusion | flops 4717056 | bytes 6303744 | tf_op jit(solution)/shard_map/while/body/eval_jaxpr/reduce_sum | solution.py:36
  187.2 3.6 %fusion.57 = f32[128,12,128]{0,2,1:T(8,128)} fusion(bf16[1024,12,128]{0,2,1:T(8,128)(2,1)S(1)} %bitcast.78, f32[12,1024,128]{2,1,0:T(8,128)S(1)} %copy-done, f32[128,12]{0,1:T(8,128)S(1)} %select_maximum_fusion.2, f32[128,12,128]{0,2,1:T(8,128)} %get-tuple-element.257, f32[128,12]{0,1:T(8,128)S(1)} %get-tuple-element.242, pred[]{:T(512)S(6)} %compare.4), kind=kOutput, calls=%fused_computation.9.clone.1 | convolution fusion | flops 407961600 | bytes 11022337 | tf_op jit(solution)/shard_map/while/body/eval_jaxpr/thk,khd->thd/dot_general | solution.py:38
  192.1 9.0 %convolution_convert_fusion = bf16[128,5120]{1,0:T(8,128)(2,1)} fusion(bf16[128,1536]{0,1:T(8,128)(2,1)S(1)} %bitcast.81, bf16[1536,5120]{1,0:T(8,128)(2,1)} %param.18), kind=kOutput, calls=%fused_computation.18 | convolution fusion | flops 2013921280 | bytes 17432576 | tf_op jit(solution)/shard_map/dot_general | solution.py:106
  204.7 34.6 %collective-permute-done.3 = bf16[256,1536]{0,1:T(8,128)(2,1)S(1)} collective-permute-done((bf16[256,1536]{0,1:T(8,128)(2,1)S(1)}, bf16[256,1536]{0,1:T(8,128)(2,1)S(1)}, u32[]{:S(2)}, u32[]{:S(2)}) %collective-permute-start.3) | collective-permute-done | bytes 786464 | tf_op jit(solution)/shard_map/ppermute | solution.py:15
  239.3 5.9 %concatenate.21 = bf16[1024,1536]{0,1:T(8,128)(2,1)} concatenate(bf16[32,1536]{0,1:T(8,128)(2,1)S(1)} %copy-done.2, bf16[32,1536]{0,1:T(8,128)(2,1)S(1)} %copy-done.4, bf16[64,1536]{0,1:T(8,128)(2,1)S(1)} %copy-done.6, bf16[128,1536]{0,1:T(8,128)(2,1)} %collective-permute-done.2, bf16[256,1536]{0,1:T(8,128)(2,1)S(1)} %collective-permute-done.3, bf16[32,1536]{0,1:T(8,128)(2,1)S(1)} %copy-done.2, ...), dimensions={0} | concatenate | bytes 6291456 | tf_op jit(solution)/shard_map/jit(_roll_dynamic)/concatenate | solution.py:19
  245.2 2.2 constant_dynamic-slice_fusion.2
  249.2 2.6 copy.32
  251.8 2.3 fusion.31
  255.1 2.3 add_convert_fusion
  (63 shorter events, 12.2 us)
Async XLA Ops:
  7.2 18.1 %copy-start.7 = (bf16[128,1536]{1,0:T(8,128)(2,1)S(1)}, bf16[128,1536]{1,0:T(8,128)(2,1)}, u32[]{:S(2)}) copy-start(bf16[128,1536]{1,0:T(8,128)(2,1)} %param.12) | copy-start | bytes 1179652
  7.2 86.6 %all-gather.4.cloned.1.call-start = ((), (), s32[]{:S(2)}) async-start(), calls=%async_computation.1 | async-start | bytes 6684672 | tf_op jit(solution)/shard_map/all_gather | solution.py:91
  9.2 151.2 %all-gather.6.cloned.1.call-start = ((), (), s32[]{:S(2)}) async-start(), calls=%async_computation.2 | async-start | bytes 6684672 | tf_op jit(solution)/shard_map/all_gather | solution.py:92
  11.2 238.0 %all-gather.8.cloned.1.call-start = ((), (), s32[]{:S(2)}) async-start(), calls=%async_computation.4 | async-start | bytes 1671168 | tf_op jit(solution)/shard_map/all_gather | solution.py:100
  12.4 148.0 %copy-start.1 = (bf16[32,1536]{0,1:T(8,128)(2,1)}, bf16[32,1536]{0,1:T(8,128)(2,1)S(1)}, u32[]{:S(2)}) copy-start(bf16[32,1536]{0,1:T(8,128)(2,1)S(1)} %copy.27) | copy-start | bytes 294916
  12.4 12.5 %collective-permute-start = (bf16[32,1536]{0,1:T(8,128)(2,1)S(1)}, bf16[32,1536]{0,1:T(8,128)(2,1)S(1)}, u32[]{:S(2)}, u32[]{:S(2)}) collective-permute-start(bf16[32,1536]{0,1:T(8,128)(2,1)S(1)} %copy.27), channel_id=1, source_target_pairs={{0,30},{2,0},{4,2},{6,4},{8,6},{10,8},{12,10},{14,12},{16,14},{18,... | collective-permute-start | bytes 294920 | tf_op jit(solution)/shard_map/ppermute | solution.py:15
  24.9 135.5 %copy-start.3 = (bf16[32,1536]{0,1:T(8,128)(2,1)}, bf16[32,1536]{0,1:T(8,128)(2,1)S(1)}, u32[]{:S(2)}) copy-start(bf16[32,1536]{0,1:T(8,128)(2,1)S(1)} %collective-permute-done) | copy-start | bytes 294916
  25.1 11.7 %collective-permute-start.1 = (bf16[64,1536]{0,1:T(8,128)(2,1)S(1)}, bf16[64,1536]{0,1:T(8,128)(2,1)S(1)}, u32[]{:S(2)}, u32[]{:S(2)}) collective-permute-start(bf16[64,1536]{0,1:T(8,128)(2,1)S(1)} %pad_maximum_fusion.1), channel_id=1, source_target_pairs={{0,28},{2,30},{4,0},{6,2},{8,4},{10,6},{12,8},{14,10},{16,12},{18,... | collective-permute-start | bytes 589832 | tf_op jit(solution)/shard_map/ppermute | solution.py:15
  25.2 229.9 %reduce-scatter.2.cloned.1.call-start = ((), (), s32[]{:S(2)}) async-start(), calls=%async_computation.3 | async-start | bytes 1966080 | tf_op jit(solution)/shard_map/reduce_scatter | solution.py:107
  36.8 123.6 %copy-start.5 = (bf16[64,1536]{0,1:T(8,128)(2,1)}, bf16[64,1536]{0,1:T(8,128)(2,1)S(1)}, u32[]{:S(2)}) copy-start(bf16[64,1536]{0,1:T(8,128)(2,1)S(1)} %collective-permute-done.1) | copy-start | bytes 589828
  37.9 163.2 %collective-permute-start.2 = (bf16[128,1536]{0,1:T(8,128)(2,1)}, bf16[128,1536]{0,1:T(8,128)(2,1)}, u32[]{:S(2)}, u32[]{:S(2)}) collective-permute-start(bf16[128,1536]{0,1:T(8,128)(2,1)} %pad_maximum_fusion.2), channel_id=1, source_target_pairs={{0,24},{2,26},{4,28},{6,30},{8,0},{10,2},{12,4},{14,6},{16,8},{18,... | collective-permute-start | bytes 1179656 | tf_op jit(solution)/shard_map/ppermute | solution.py:15
  167.8 4.0 %copy-start.9 = (f32[128,12]{0,1:T(8,128)S(1)}, f32[128,12]{0,1:T(8,128)}, u32[]{:S(2)}) copy-start(f32[128,12]{0,1:T(8,128)} %get-tuple-element.256) | copy-start | bytes 18436 | tf_op jit(solution)/shard_map/while
  167.8 4.7 %copy-start = (f32[12,1024,128]{2,1,0:T(8,128)S(1)}, f32[12,1024,128]{2,1,0:T(8,128)}, u32[]{:S(2)}) copy-start(f32[12,1024,128]{2,1,0:T(8,128)} %get-tuple-element.239) | copy-start | bytes 18874372 | tf_op jit(solution)/shard_map/while
  171.8 3.1 %copy-start.10 = (f32[128,12]{0,1:T(8,128)}, f32[128,12]{0,1:T(8,128)S(1)}, u32[]{:S(2)}) copy-start(f32[128,12]{0,1:T(8,128)S(1)} %get-tuple-element.267) | copy-start | bytes 18436 | tf_op jit(solution)/shard_map/while
  182.4 4.0 %copy-start.9 = (f32[128,12]{0,1:T(8,128)S(1)}, f32[128,12]{0,1:T(8,128)}, u32[]{:S(2)}) copy-start(f32[128,12]{0,1:T(8,128)} %get-tuple-element.256) | copy-start | bytes 18436 | tf_op jit(solution)/shard_map/while
  182.4 4.8 %copy-start = (f32[12,1024,128]{2,1,0:T(8,128)S(1)}, f32[12,1024,128]{2,1,0:T(8,128)}, u32[]{:S(2)}) copy-start(f32[12,1024,128]{2,1,0:T(8,128)} %get-tuple-element.239) | copy-start | bytes 18874372 | tf_op jit(solution)/shard_map/while
  186.4 4.4 %copy-start.10 = (f32[128,12]{0,1:T(8,128)}, f32[128,12]{0,1:T(8,128)S(1)}, u32[]{:S(2)}) copy-start(f32[128,12]{0,1:T(8,128)S(1)} %get-tuple-element.267) | copy-start | bytes 18436 | tf_op jit(solution)/shard_map/while
  192.1 9.1 %copy-start.2 = (bf16[32,1536]{0,1:T(8,128)(2,1)S(1)}, bf16[32,1536]{0,1:T(8,128)(2,1)}, u32[]{:S(2)}) copy-start(bf16[32,1536]{0,1:T(8,128)(2,1)} %copy-done.1) | copy-start | bytes 294916
  192.1 9.1 %copy-start.4 = (bf16[32,1536]{0,1:T(8,128)(2,1)S(1)}, bf16[32,1536]{0,1:T(8,128)(2,1)}, u32[]{:S(2)}) copy-start(bf16[32,1536]{0,1:T(8,128)(2,1)} %copy-done.3) | copy-start | bytes 294916
  192.1 9.1 %copy-start.6 = (bf16[64,1536]{0,1:T(8,128)(2,1)S(1)}, bf16[64,1536]{0,1:T(8,128)(2,1)}, u32[]{:S(2)}) copy-start(bf16[64,1536]{0,1:T(8,128)(2,1)} %copy-done.5) | copy-start | bytes 589828
  201.1 3.4 %copy-start.8 = (bf16[128,1536]{1,0:T(8,128)(2,1)S(1)}, bf16[128,1536]{1,0:T(8,128)(2,1)}, u32[]{:S(2)}) copy-start(bf16[128,1536]{1,0:T(8,128)(2,1)} %param.15) | copy-start | bytes 1179652
  202.8 36.4 %collective-permute-start.3 = (bf16[256,1536]{0,1:T(8,128)(2,1)S(1)}, bf16[256,1536]{0,1:T(8,128)(2,1)S(1)}, u32[]{:S(2)}, u32[]{:S(2)}) collective-permute-start(bf16[256,1536]{0,1:T(8,128)(2,1)S(1)} %pad_maximum_fusion), channel_id=1, source_target_pairs={{0,16},{2,18},{4,20},{6,22},{8,24},{10,26},{12,28},{14,30},{16,0},... | collective-permute-start | bytes 2359304 | tf_op jit(solution)/shard_map/ppermute | solution.py:15
Sparse Core Ops, SparseCore 0:
  10.7 82.9 all-gather.3
  96.5 63.8 all-gather.5
  162.7 37.8 all-gather.7
  202.6 22.0 reduce-scatter.1
